TPU v7x, 32 devices: a whole 2x2x4 slice. The times are simulated.
32 devices in a mesh: blk: 4 (over x, core), uly: 8 (over z, y).
Axes of the slice: x: 2, y: 2, z: 4, core: 2. Of those that a mesh axis runs over, the one named last changes fastest.
Arguments:
- query_rows: bfloat16 [4096, 512], P(('blk', 'uly')), may hold values from -6 to 6
- key_rows: bfloat16 [4096, 512], P(('blk', 'uly')), may hold values from -6 to 6
- value_rows: bfloat16 [4096, 512], P(('blk', 'uly')), may hold values from -6 to 6
- out_grad: bfloat16 [4096, 512], P(('blk', 'uly')), may hold values from -6 to 6
- block_lists: int32 [64, 8], P('blk'), may hold values from 0 to 63, as said below
- block_counts: int32 [64], P('blk'), may hold values from 1 to 8
Outputs:
- attended: bfloat16 [4096, 512], P(('blk', 'uly'))
- query_gradient: bfloat16 [4096, 512], P(('blk', 'uly'))
- key_grad: bfloat16 [4096, 512], P(('blk', 'uly'))
- value_grad: bfloat16 [4096, 512], P(('blk', 'uly'))
Inputs may be any that keep to these rules, and one draw needn't show every extreme that they name: `block_lists`: row b lists key blocks of query block b: entry 0 is b, entries 1 to block_counts[b] - 1 are distinct blocks other than b, and the remaining entries equal b.
All inputs are finite; a program needn't handle non-finite values.
Results may differ from a plain program's by a relative error of at most 0.02.
Values may be sent and summed in bfloat16 or wider, within the bound.
A program may use at most 128 MiB of HBM per device.

v0:
```python
import math
import jax
import jax.numpy as jnp
from jax import lax
from jax.sharding import PartitionSpec as P

HDIM = 64
BLK = 64
KSEL = 8


def fetch_sets(pair_blocks, list_group, count_group):
    picked = pair_blocks[list_group]
    usable = (jnp.arange(KSEL)[None, :] < count_group[:, None])[:, None, None, :, None]
    return (picked[..., :HDIM], picked[..., HDIM:], usable)


def probabilities(query_group, gathered_key_blocks, usable):
    logit_matrix = jnp.einsum(
        "gqhd,gjkhd->gqhjk", query_group, gathered_key_blocks, preferred_element_type=jnp.float32
    ) * (1.0 / math.sqrt(HDIM))
    row_max = jnp.max(jnp.where(usable, logit_matrix, -1e30), axis=(3, 4), keepdims=True)
    weights = jnp.where(usable, jnp.exp(logit_matrix - row_max), 0.0)
    return weights / jnp.sum(weights, axis=(3, 4), keepdims=True)


def attend(reduced_precision, gathered_value_blocks):
    return jnp.einsum(
        "gqhjk,gjkhd->gqhd",
        reduced_precision,
        gathered_value_blocks,
        preferred_element_type=jnp.float32,
    ).astype(jnp.bfloat16)


def backward_group(
    gathered_key_blocks,
    gathered_value_blocks,
    query_group,
    grad_group,
    out_group,
    probability,
    reduced_precision,
):
    softmax_scale = 1.0 / math.sqrt(HDIM)
    delta = jnp.sum(grad_group.astype(jnp.float32) * out_group.astype(jnp.float32), axis=-1)[
        ..., None, None
    ]
    probability_gradient = jnp.einsum(
        "gqhd,gjkhd->gqhjk", grad_group, gathered_value_blocks, preferred_element_type=jnp.float32
    )
    score_gradient = (probability * (probability_gradient - delta)).astype(jnp.bfloat16)
    query_gradient = (
        jnp.einsum(
            "gqhjk,gjkhd->gqhd",
            score_gradient,
            gathered_key_blocks,
            preferred_element_type=jnp.float32,
        )
        * softmax_scale
    ).astype(jnp.bfloat16)
    key_contribution = (
        jnp.einsum(
            "gqhjk,gqhd->gjkhd", score_gradient, query_group, preferred_element_type=jnp.float32
        )
        * softmax_scale
    )
    value_contribution = jnp.einsum(
        "gqhjk,gqhd->gjkhd", reduced_precision, grad_group, preferred_element_type=jnp.float32
    )
    return (query_gradient, jnp.concatenate([key_contribution, value_contribution], axis=-1))


def on_device(query_rows, key_rows, value_rows, out_grad, block_lists, block_counts):
    tok_rows = query_rows.shape[0]
    width = query_rows.shape[1]
    heads = width // HDIM
    query_heads = query_rows.reshape(tok_rows, heads, HDIM)
    grad_heads = out_grad.reshape(tok_rows, heads, HDIM)
    pair_heads = jnp.concatenate(
        [key_rows.reshape(tok_rows, heads, HDIM), value_rows.reshape(tok_rows, heads, HDIM)], axis=2
    )
    seg_query, seg_pair, seg_grad = (
        lax.all_to_all(query_heads, "uly", split_axis=1, concat_axis=0, tiled=True),
        lax.all_to_all(pair_heads, "uly", split_axis=1, concat_axis=0, tiled=True),
        lax.all_to_all(grad_heads, "uly", split_axis=1, concat_axis=0, tiled=True),
    )
    all_pairs = lax.all_gather(seg_pair, "blk", axis=0, tiled=True)
    seg_rows = seg_query.shape[0]
    head_local = seg_query.shape[1]
    local_blocks = seg_rows // BLK
    group_size = math.gcd(16, local_blocks)
    groups = local_blocks // group_size
    pair_blocks = all_pairs.reshape(-1, BLK, head_local, 2 * HDIM)
    query_groups = seg_query.reshape(groups, group_size, BLK, head_local, HDIM)
    grad_groups = seg_grad.reshape(groups, group_size, BLK, head_local, HDIM)
    list_groups = block_lists.reshape(groups, group_size, KSEL)
    count_groups = block_counts.reshape(groups, group_size)
    empty = jnp.zeros(pair_blocks.shape, jnp.float32)

    def joint_turn(accum, operands):
        query_group, grad_group, list_group, count_group = operands
        gathered_key_blocks, gathered_value_blocks, usable = fetch_sets(
            pair_blocks, list_group, count_group
        )
        probability = probabilities(query_group, gathered_key_blocks, usable)
        reduced_precision = probability.astype(jnp.bfloat16)
        out_group = attend(reduced_precision, gathered_value_blocks)
        query_gradient, pair_terms = backward_group(
            gathered_key_blocks,
            gathered_value_blocks,
            query_group,
            grad_group,
            out_group,
            probability,
            reduced_precision,
        )
        return (accum.at[list_group].add(pair_terms), (out_group, query_gradient))

    accum, (out_groups, query_parts) = lax.scan(
        joint_turn, empty, (query_groups, grad_groups, list_groups, count_groups)
    )
    accum_rows = accum.reshape(-1, head_local, 2 * HDIM)
    summed = lax.psum_scatter(accum_rows, "blk", scatter_dimension=0, tiled=True)
    pair_grad = summed.astype(jnp.bfloat16)
    out_seg = out_groups.reshape(seg_rows, head_local, HDIM)
    query_seg = query_parts.reshape(seg_rows, head_local, HDIM)
    out_back, query_back, pair_back = (
        lax.all_to_all(out_seg, "uly", split_axis=0, concat_axis=1, tiled=True),
        lax.all_to_all(query_seg, "uly", split_axis=0, concat_axis=1, tiled=True),
        lax.all_to_all(pair_grad, "uly", split_axis=0, concat_axis=1, tiled=True),
    )
    return (
        out_back.reshape(tok_rows, width),
        query_back.reshape(tok_rows, width),
        pair_back[..., :HDIM].reshape(tok_rows, width),
        pair_back[..., HDIM:].reshape(tok_rows, width),
    )


def solution(mesh):
    placed = (
        P(("blk", "uly"), None),
        P(("blk", "uly"), None),
        P(("blk", "uly"), None),
        P(("blk", "uly"), None),
        P("blk", None),
        P("blk"),
    )
    return jax.shard_map(
        on_device,
        mesh=mesh,
        in_specs=placed,
        out_specs=(
            P(("blk", "uly"), None),
            P(("blk", "uly"), None),
            P(("blk", "uly"), None),
            P(("blk", "uly"), None),
        ),
        check_vma=False,
    )
```

profile of v0, /device:TPU:0, one launch (start us, length us, event | category | flops | bytes accessed | tf_op | source)
XLA Modules:
  0.0 136.0 jit_solution(9518933461510708066)
XLA Ops:
  7.2 1.0 copy.69
  8.2 1.0 copy.70
  9.3 16.0 %all_to_all.96 = bf16[128,8,128]{0,2,1:T(8,128)(2,1)S(1)} all-to-all(bf16[128,8,128]{0,2,1:T(8,128)(2,1)S(1)} %pad_maximum_fusion.1), channel_id=1, replica_groups=mesh['blk'=4,'uly'=8] {'uly'}, dimensions={1} | all-to-all | bytes 524288 | tf_op jit(solution)/shard_map/all_to_all | solution.py:85
  25.3 0.9 copy.71
  26.2 1.7 %copy.73 = bf16[128,512]{0,1:T(8,128)(2,1)} copy(bf16[128,512]{1,0:T(8,128)(2,1)} %param.6) | data formatting | bytes 262144 | tf_op args[0]
  27.8 3.6 %all-to-all-start.1 = ((bf16[128,8,64]{0,2,1:T(8,128)(2,1)}), bf16[128,8,64]{0,2,1:T(8,128)(2,1)S(1)}, u32[]{:S(2)}, u32[]{:S(2)}) async-start(bf16[128,8,64]{0,2,1:T(8,128)(2,1)} %bitcast.9), calls=%async_computation.1 | async-start | bytes 262144 | tf_op jit(solution)/shard_map/all_to_all | solution.py:84
  32.3 1.7 %copy.81 = bf16[128,512]{0,1:T(8,128)(2,1)} copy(bf16[128,512]{1,0:T(8,128)(2,1)} %param.9) | data formatting | bytes 262144 | tf_op args[3]
  34.0 4.8 %all-to-all-done.1 = bf16[128,8,64]{0,2,1:T(8,128)(2,1)S(1)} async-done(((bf16[128,8,64]{0,2,1:T(8,128)(2,1)}), bf16[128,8,64]{0,2,1:T(8,128)(2,1)S(1)}, u32[]{:S(2)}, u32[]{:S(2)}) %all-to-all-start.1) | async-done | bytes 131104 | tf_op jit(solution)/shard_map/all_to_all | solution.py:84
  38.8 3.4 %all-to-all-start.3 = ((bf16[128,8,64]{0,2,1:T(8,128)(2,1)}), bf16[128,8,64]{0,2,1:T(8,128)(2,1)S(1)}, u32[]{:S(2)}, u32[]{:S(2)}) async-start(bf16[128,8,64]{0,2,1:T(8,128)(2,1)} %bitcast.24), calls=%async_computation.3 | async-start | bytes 262144 | tf_op jit(solution)/shard_map/all_to_all | solution.py:86
  43.1 6.3 %all-to-all-done.3 = bf16[128,8,64]{0,2,1:T(8,128)(2,1)S(1)} async-done(((bf16[128,8,64]{0,2,1:T(8,128)(2,1)}), bf16[128,8,64]{0,2,1:T(8,128)(2,1)S(1)}, u32[]{:S(2)}, u32[]{:S(2)}) %all-to-all-start.3) | async-done | bytes 131104 | tf_op jit(solution)/shard_map/all_to_all | solution.py:86
  50.0 2.2 %gather_fusion = bf16[128,64,128]{2,1,0:T(8,128)(2,1)S(1)} fusion(bf16[64,64,128]{2,1,0:T(8,128)(2,1)} %bitcast.208, s32[1024]{0:T(1024)S(1)} %pad_clamp_fusion), kind=kCustom, calls=%fused_computation | custom fusion | bytes 4194816 | tf_op jit(solution)/shard_map/while/body/eval_jaxpr/gather | solution.py:13
  52.2 1.0 fusion.1
  53.2 1.1 bitcast_reduce_fusion
  54.4 2.3 %fusion.33 = (f32[16,64]{1,0:T(8,128)S(1)}, bf16[16,64,1,64]{1,3,0,2:T(8,128)(2,1)S(1)}) fusion(f32[16,64,1,64]{1,0,3,2:T(8,128)S(1)} %reshape.172, f32[16,64]{1,0:T(8,128)S(1)} %bitcast_reduce_fusion, f32[16,64]{1,0:T(8,128)S(1)} %get-tuple-element.45, f32[16,8,64,64]{3,2,1,0:T(8,128)S(1)} %get-tuple-element.46, pred[16,8]{1,0:T(8,128)(4,1)S(1)} %iota_compare_fusion, ...), kind=kOutput, calls=%fused_computation.33 | convolution fusion | flops 69991424 | bytes 4599936 | tf_op jit(solution)/shard_map/while/body/eval_jaxpr/gqhjk,gjkhd->gqhd/dot_general | solution.py:28
  56.7 1.3 convolution_bitcast_fusion
  57.9 1.9 %fusion = bf16[16,64,1,8,64]{1,4,3,0,2:T(8,128)(2,1)S(1)} fusion(bf16[16,64,64,1]{2,1,3,0:T(8,128)(2,1)S(1)} %bitcast.231, f32[16,64]{1,0:T(8,128)S(1)} %get-tuple-element.47, f32[16,64]{1,0:T(8,128)S(1)} %bitcast_reduce_fusion, f32[16,64]{1,0:T(8,128)S(1)} %get-tuple-element.45, f32[16,8,64,64]{3,2,1,0:T(8,128)S(1)} %get-tuple-element.46, ...), kind=kOutput, calls=%fused_computation.4 | convolution fusion | flops 70778880 | bytes 5386368 | tf_op jit(solution)/shard_map/while/body/eval_jaxpr/gqhd,gjkhd->gqhjk/dot_general | solution.py:49
  60.5 3.1 %pad_maximum_fusion = f32[16,8,64,1,128]{4,2,1,0,3:T(8,128)} fusion(f32[16,8,64,1,64]{4,2,1,0,3:T(8,128)S(1)} %convolution_bitcast_fusion, f32[16,8,64,1,64]{4,2,1,0,3:T(8,128)S(1)} %multiply_bitcast_fusion), kind=kLoop, calls=%fused_computation.2 | loop fusion | flops 1048576 | bytes 8388608 | tf_op jit(solution)/shard_map/while/body/eval_jaxpr/concatenate | solution.py:71
  63.8 13.5 %scatter_fusion = f32[64,64,128]{2,1,0:T(8,128)S(1)} fusion(f32[64,64,128]{2,1,0:T(8,128)S(1)} %broadcast.65, s32[128]{0:T(128)S(1)} %reshape.177, f32[128,64,128]{2,1,0:T(8,128)} %bitcast.207), kind=kCustom, calls=%fused_computation.1 | custom fusion | flops 1048576 | bytes 12583424 | tf_op jit(solution)/shard_map/while/body/eval_jaxpr/scatter-add | solution.py:118
  77.4 1.3 copy-done
  79.6 2.3 %reduce.4 = bf16[1024,64]{1,0:T(8,128)(2,1)S(1)} reduce(bf16[1024,1,64]{2,1,0:T(2,128)(2,1)S(1)} %reshape.205, bf16[]{:T(256)} %broadcast.90), dimensions={1}, to_apply=%reshape.205.reduce_sub_computation | reduce | bytes 262146 | tf_op jit(solution)/shard_map/reshape | solution.py:126
  81.8 0.9 reshape.207
  82.7 3.6 %all-to-all-start.2 = ((bf16[8,2,4096]{2,1,0:T(2,128)(2,1)}), bf16[8,2,4096]{2,1,0:T(2,128)(2,1)S(1)}, u32[]{:S(2)}, u32[]{:S(2)}) async-start(bf16[8,2,4096]{2,1,0:T(2,128)(2,1)} %reshape.207), calls=%async_computation.2 | async-start | bytes 262144 | tf_op jit(solution)/shard_map/all_to_all | solution.py:129
  86.3 3.0 %fusion.27 = bf16[16,64,1,64]{1,3,0,2:T(8,128)(2,1)S(1)} fusion(bf16[16,64,1,8,64]{1,4,3,0,2:T(8,128)(2,1)} %copy-done.1, bf16[16,8,64,1,128]{4,2,1,0,3:T(8,128)(2,1)} %bitcast.213), kind=kOutput, calls=%fused_computation.30 | convolution fusion | flops 67239936 | bytes 3276800 | tf_op jit(solution)/shard_map/while/body/eval_jaxpr/gqhjk,gjkhd->gqhd/dot_general | solution.py:54
  89.7 2.3 %reduce.5 = bf16[1024,64]{1,0:T(8,128)(2,1)S(1)} reduce(bf16[1024,1,64]{2,1,0:T(2,128)(2,1)S(1)} %reshape.206, bf16[]{:T(256)} %broadcast.90), dimensions={1}, to_apply=%reshape.206.reduce_sub_computation | reduce | bytes 262146 | tf_op jit(solution)/shard_map/reshape | solution.py:127
  92.0 0.9 reshape.209
  93.4 5.2 %all-to-all-start.4 = ((bf16[8,2,4096]{2,1,0:T(2,128)(2,1)}), bf16[8,2,4096]{2,1,0:T(2,128)(2,1)S(1)}, u32[]{:S(2)}, u32[]{:S(2)}) async-start(bf16[8,2,4096]{2,1,0:T(2,128)(2,1)} %reshape.209), calls=%async_computation.4 | async-start | bytes 262144 | tf_op jit(solution)/shard_map/all_to_all | solution.py:130
  98.6 9.4 %reduce-scatter.2.cloned.1.call-done = f32[1024,1,128]{2,1,0:T(1,128)} async-done(((f32[4096,1,128]{2,1,0:T(1,128)}), f32[1024,1,128]{2,1,0:T(1,128)}) %reduce-scatter.2.cloned.1.call-update) | async-done | bytes 524304 | tf_op jit(solution)/shard_map/reduce_scatter | solution.py:124
  108.1 1.4 %convert_element_type.61 = bf16[1024,1,128]{2,1,0:T(2,128)(2,1)S(1)} convert(f32[1024,1,128]{2,1,0:T(1,128)} %reduce-scatter.2.cloned.1.call-done) | non-fusion elementwise | flops 131072 | bytes 786432 | tf_op jit(solution)/shard_map/convert_element_type | solution.py:125
  109.5 2.2 %reduce.6 = bf16[1024,128]{1,0:T(8,128)(2,1)S(1)} reduce(bf16[1024,1,128]{2,1,0:T(2,128)(2,1)S(1)} %convert_element_type.61, bf16[]{:T(256)} %broadcast.90), dimensions={1}, to_apply=%convert_element_type.61.reduce_sub_computation | reduce | bytes 524290 | tf_op jit(solution)/shard_map/convert_element_type | solution.py:125
  112.4 5.5 %all-to-all-start.5 = ((bf16[8,2,8192]{2,1,0:T(2,128)(2,1)}), bf16[8,2,8192]{2,1,0:T(2,128)(2,1)S(1)}, u32[]{:S(2)}, u32[]{:S(2)}) async-start(bf16[8,2,8192]{2,1,0:T(2,128)(2,1)} %reshape.211), calls=%async_computation.6 | async-start | bytes 524288 | tf_op jit(solution)/shard_map/all_to_all | solution.py:131
  120.9 6.0 %all-to-all-done.5 = bf16[8,2,8192]{2,1,0:T(2,128)(2,1)S(1)} async-done(((bf16[8,2,8192]{2,1,0:T(2,128)(2,1)}), bf16[8,2,8192]{2,1,0:T(2,128)(2,1)S(1)}, u32[]{:S(2)}, u32[]{:S(2)}) %all-to-all-start.5) | async-done | bytes 262176 | tf_op jit(solution)/shard_map/all_to_all | solution.py:131
  127.5 0.8 copy.96
  (47 shorter events, 10.2 us)
Async XLA Ops:
  7.2 42.8 %all-gather.2.cloned.1.call-start = ((), (), s32[]{:S(2)}) async-start(), calls=%async_computation.7 | async-start | bytes 1310720 | tf_op jit(solution)/shard_map/all_gather | solution.py:88
  27.8 10.9 %all-to-all-start.1 = ((bf16[128,8,64]{0,2,1:T(8,128)(2,1)}), bf16[128,8,64]{0,2,1:T(8,128)(2,1)S(1)}, u32[]{:S(2)}, u32[]{:S(2)}) async-start(bf16[128,8,64]{0,2,1:T(8,128)(2,1)} %bitcast.9), calls=%async_computation.1 | async-start | bytes 262144 | tf_op jit(solution)/shard_map/all_to_all | solution.py:84
  38.8 10.7 %all-to-all-start.3 = ((bf16[128,8,64]{0,2,1:T(8,128)(2,1)}), bf16[128,8,64]{0,2,1:T(8,128)(2,1)S(1)}, u32[]{:S(2)}, u32[]{:S(2)}) async-start(bf16[128,8,64]{0,2,1:T(8,128)(2,1)} %bitcast.24), calls=%async_computation.3 | async-start | bytes 262144 | tf_op jit(solution)/shard_map/all_to_all | solution.py:86
  42.2 65.9 %reduce-scatter.2.cloned.1.call-start = ((), (), s32[]{:S(2)}) async-start(), calls=%async_computation.8 | async-start | bytes 2621440 | tf_op jit(solution)/shard_map/reduce_scatter | solution.py:124
  52.2 5.7 %copy-start.2 = (bf16[128,64,128]{2,1,0:T(8,128)(2,1)}, bf16[128,64,128]{2,1,0:T(8,128)(2,1)S(1)}, u32[]{:S(2)}) copy-start(bf16[128,64,128]{2,1,0:T(8,128)(2,1)S(1)} %gather_fusion) | copy-start | bytes 6291460
  59.8 3.8 %copy-start.1 = (bf16[16,64,1,8,64]{1,4,3,0,2:T(8,128)(2,1)}, bf16[16,64,1,8,64]{1,4,3,0,2:T(8,128)(2,1)S(1)}, u32[]{:S(2)}) copy-start(bf16[16,64,1,8,64]{1,4,3,0,2:T(8,128)(2,1)S(1)} %fusion) | copy-start | bytes 3145732
  77.3 1.4 copy-start
  82.7 10.7 %all-to-all-start.2 = ((bf16[8,2,4096]{2,1,0:T(2,128)(2,1)}), bf16[8,2,4096]{2,1,0:T(2,128)(2,1)S(1)}, u32[]{:S(2)}, u32[]{:S(2)}) async-start(bf16[8,2,4096]{2,1,0:T(2,128)(2,1)} %reshape.207), calls=%async_computation.2 | async-start | bytes 262144 | tf_op jit(solution)/shard_map/all_to_all | solution.py:129
  93.4 19.0 %all-to-all-start.4 = ((bf16[8,2,4096]{2,1,0:T(2,128)(2,1)}), bf16[8,2,4096]{2,1,0:T(2,128)(2,1)S(1)}, u32[]{:S(2)}, u32[]{:S(2)}) async-start(bf16[8,2,4096]{2,1,0:T(2,128)(2,1)} %reshape.209), calls=%async_computation.4 | async-start | bytes 262144 | tf_op jit(solution)/shard_map/all_to_all | solution.py:130
  112.4 14.4 %all-to-all-start.5 = ((bf16[8,2,8192]{2,1,0:T(2,128)(2,1)}), bf16[8,2,8192]{2,1,0:T(2,128)(2,1)S(1)}, u32[]{:S(2)}, u32[]{:S(2)}) async-start(bf16[8,2,8192]{2,1,0:T(2,128)(2,1)} %reshape.211), calls=%async_computation.6 | async-start | bytes 524288 | tf_op jit(solution)/shard_map/all_to_all | solution.py:131
Sparse Core Ops, SparseCore 0:
  26.3 15.7 all-gather.1
  78.8 29.1 reduce-scatter.1
where the time goes:
time: 137 us; the launch traced here: 136 us
  other arithmetic  27.3 us (20%)
  waiting for transfers between devices  27 us (20%)
  starting transfers between devices  21.3 us (16%)
  local copies, waits for them, and re-layouts  19.7 us (14%)
  blocking collectives  16 us (12%)
  between operations  14.4 us (11%)
  matrix products  10.2 us (7%)
    all_to_all x1, blocking collectives, on_device(): lax.all_to_all(pair_heads, 'uly', split_axis=1, concat_axis=0, tiled=True)  16 us
    scatter-add x1, other arithmetic, joint_turn(): return (accum.at[list_group].add(pair_terms), (out_group, query_gradient))  13.5 us
    unnamed x23, local copies, waits for them, and re-layouts  13.4 us
    reduce_scatter x1, waiting for transfers between devices, on_device(): lax.psum_scatter(accum_rows, 'blk', scatter_dimension=0, tiled=True)  9.43 us
    all_to_all x1, waiting for transfers between devices, on_device(): lax.all_to_all(grad_heads, 'uly', split_axis=1, concat_axis=0, tiled=True)  6.3 us
    all_to_all x1, waiting for transfers between devices, on_device(): lax.all_to_all(pair_grad, 'uly', split_axis=0, concat_axis=1, tiled=True)  5.97 us
    all_to_all x1, starting transfers between devices, on_device(): lax.all_to_all(pair_grad, 'uly', split_axis=0, concat_axis=1, tiled=True)  5.52 us
    all_to_all x1, starting transfers between devices, on_device(): lax.all_to_all(query_seg, 'uly', split_axis=0, concat_axis=1, tiled=True)  5.22 us
  transfers between devices with their start and end apart: 7, of which 5 were waited for; matrix products, arithmetic and copies ran while one was open for 17% of the time, Pallas kernels for 0%

commit v1 on v0

--- a/solution.py
+++ b/solution.py
@@ -7,6 +7,29 @@
 HDIM = 64
 BLK = 64
 KSEL = 8
+
+
+def in_blocks(shard, dim, length):
+    lengths = shard.shape
+    tiles = shard.reshape(*lengths[:dim], length, lengths[dim] // length, *lengths[dim + 1 :])
+    return jnp.moveaxis(tiles, dim, 0)
+
+
+def in_order(blocks, dim):
+    blocks = jnp.moveaxis(blocks, 0, dim)
+    shape = blocks.shape
+    return blocks.reshape(*shape[:dim], shape[dim] * shape[dim + 1], *shape[dim + 2 :])
+
+
+def exchange_directly(array, axis, split_dim, concat_dim):
+    size, index = (lax.axis_size(axis), lax.axis_index(axis))
+    blocks = in_blocks(array, split_dim, size)
+    outs = [blocks[index]]
+    for turn in range(1, size):
+        sent = blocks[(index + turn) % size]
+        outs.append(lax.ppermute(sent, axis, [(i, (i + turn) % size) for i in range(size)]))
+    blocks = jnp.stack(outs)[(index - jnp.arange(size)) % size]
+    return in_order(blocks, concat_dim)
 
 
 def fetch_sets(pair_blocks, list_group, count_group):
@@ -81,7 +104,7 @@
         [key_rows.reshape(tok_rows, heads, HDIM), value_rows.reshape(tok_rows, heads, HDIM)], axis=2
     )
     seg_query, seg_pair, seg_grad = (
-        lax.all_to_all(query_heads, "uly", split_axis=1, concat_axis=0, tiled=True),
+        exchange_directly(query_heads, "uly", 1, 0),
         lax.all_to_all(pair_heads, "uly", split_axis=1, concat_axis=0, tiled=True),
         lax.all_to_all(grad_heads, "uly", split_axis=1, concat_axis=0, tiled=True),
     )

time: 137 us -> 150 us (1.095)
  starting transfers between devices: 21.3 us -> 40 us
  blocking collectives: 16 us -> 0 us
  waiting for transfers between devices: 27 us -> 34.6 us
    all_to_all x1 -> x0, blocking collectives: 16 us -> none  [on_device(): lax.all_to_all(pair_heads, 'uly', split_axis=1, concat_axis=0, tiled=True)]
    ppermute x0 -> x7, starting transfers between devices: none -> 15.9 us  [exchange_directly(): lax.ppermute(sent, axis, [(i, (i + turn) % size) for i in range(size)])]
    all_gather x1, waiting for transfers between devices: 0.02 us -> 12.3 us  [on_device(): all_pairs = lax.all_gather(seg_pair, 'blk', axis=0, tiled=True)]
    all_to_all x1, waiting for transfers between devices: 6.3 us -> 0.01 us  [on_device(): lax.all_to_all(grad_heads, 'uly', split_axis=1, concat_axis=0, tiled=True)]
    ppermute x0 -> x7, waiting for transfers between devices: none -> 2.93 us  [exchange_directly(): lax.ppermute(sent, axis, [(i, (i + turn) % size) for i in range(size)])]
    all_to_all x1, starting transfers between devices: 3.56 us -> 5.52 us  [on_device(): lax.all_to_all(out_seg, 'uly', split_axis=0, concat_axis=1, tiled=True)]
    all_to_all x1, waiting for transfers between devices: 4.76 us -> 3.07 us  [on_device(): lax.all_to_all(pair_heads, 'uly', split_axis=1, concat_axis=0, tiled=True)]
    unnamed x23 -> x32, local copies, waits for them, and re-layouts: 13.4 us -> 13.4 us
  transfers between devices with their start and end apart: 7 -> 14, of which waited for: 5 -> 6; matrix products, arithmetic and copies ran while one was open for 17% -> 18% of each run, Pallas kernels for 0% -> 0%
where the time goes in v1:
time: 150 us; the launch traced here: 149 us
  starting transfers between devices  40 us (27%)
  waiting for transfers between devices  34.6 us (23%)
  other arithmetic  28.5 us (19%)
  local copies, waits for them, and re-layouts  20.4 us (14%)
  between operations  14.6 us (10%)
  matrix products  10.8 us (7%)
    ppermute x7, starting transfers between devices, exchange_directly(): lax.ppermute(sent, axis, [(i, (i + turn) % size) for i in range(size)])  15.9 us
    scatter-add x1, other arithmetic, joint_turn(): return (accum.at[list_group].add(pair_terms), (out_group, query_gradient))  13.5 us
    unnamed x32, local copies, waits for them, and re-layouts  13.4 us
    all_gather x1, waiting for transfers between devices, on_device(): all_pairs = lax.all_gather(seg_pair, 'blk', axis=0, tiled=True)  12.3 us
    reduce_scatter x1, waiting for transfers between devices, on_device(): lax.psum_scatter(accum_rows, 'blk', scatter_dimension=0, tiled=True)  9.48 us
    all_to_all x1, waiting for transfers between devices, on_device(): lax.all_to_all(pair_grad, 'uly', split_axis=0, concat_axis=1, tiled=True)  5.98 us
    all_to_all x1, starting transfers between devices, on_device(): lax.all_to_all(pair_grad, 'uly', split_axis=0, concat_axis=1, tiled=True)  5.52 us
    all_to_all x1, starting transfers between devices, on_device(): lax.all_to_all(out_seg, 'uly', split_axis=0, concat_axis=1, tiled=True)  5.52 us
  transfers between devices with their start and end apart: 14, of which 6 were waited for; matrix products, arithmetic and copies ran while one was open for 18% of the time, Pallas kernels for 0%

profile of v1, /device:TPU:0, one launch (start us, length us, event | category | flops | bytes accessed | tf_op | source)
XLA Modules:
  0.0 148.9 jit_solution(8262365117448626899)
XLA Ops:
  7.3 1.0 copy.99
  8.3 6.1 %collective-permute-start.6 = (bf16[128,1,64]{0,2,1:T(8,128)(2,1)S(1)}, bf16[128,1,64]{0,2,1:T(8,128)(2,1)S(1)}, u32[]{:S(2)}, u32[]{:S(2)}) collective-permute-start(bf16[128,1,64]{0,2,1:T(8,128)(2,1)S(1)} %get-tuple-element.49), channel_id=1, source_target_pairs={{0,7},{1,0},{2,1},{3,2},{4,3},{5,4},{6,5},{7,6},{8,15},{9,8},{10,9... | collective-permute-start | bytes 49160 | tf_op jit(solution)/shard_map/ppermute | solution.py:30
  14.9 3.0 %collective-permute-start.3 = (bf16[128,1,64]{0,2,1:T(8,128)(2,1)S(1)}, bf16[128,1,64]{0,2,1:T(8,128)(2,1)S(1)}, u32[]{:S(2)}, u32[]{:S(2)}) collective-permute-start(bf16[128,1,64]{0,2,1:T(8,128)(2,1)S(1)} %get-tuple-element.52), channel_id=1, source_target_pairs={{0,4},{1,5},{2,6},{3,7},{4,0},{5,1},{6,2},{7,3},{8,12},{9,13},{10,... | collective-permute-start | bytes 49160 | tf_op jit(solution)/shard_map/ppermute | solution.py:30
  17.8 1.5 %collective-permute-start = (bf16[128,1,64]{0,2,1:T(8,128)(2,1)S(1)}, bf16[128,1,64]{0,2,1:T(8,128)(2,1)S(1)}, u32[]{:S(2)}, u32[]{:S(2)}) collective-permute-start(bf16[128,1,64]{0,2,1:T(8,128)(2,1)S(1)} %get-tuple-element.55), channel_id=1, source_target_pairs={{0,1},{1,2},{2,3},{3,4},{4,5},{5,6},{6,7},{7,0},{8,9},{9,10},{10,1... | collective-permute-start | bytes 49160 | tf_op jit(solution)/shard_map/ppermute | solution.py:30
  19.4 1.0 copy.95
  20.4 1.0 copy.96
  22.1 4.5 %all-to-all-start = ((bf16[128,8,128]{0,2,1:T(8,128)(2,1)}), bf16[128,8,128]{0,2,1:T(8,128)(2,1)S(1)}, u32[]{:S(2)}, u32[]{:S(2)}) async-start(bf16[128,8,128]{0,2,1:T(8,128)(2,1)} %pad_maximum_fusion.1), calls=%async_computation | async-start | bytes 524288 | tf_op jit(solution)/shard_map/all_to_all | solution.py:108
  28.3 1.7 %copy.108 = bf16[128,512]{0,1:T(8,128)(2,1)} copy(bf16[128,512]{1,0:T(8,128)(2,1)} %param.9) | data formatting | bytes 262144 | tf_op args[3]
  29.9 2.0 %collective-permute-start.1 = (bf16[128,1,64]{0,2,1:T(8,128)(2,1)S(1)}, bf16[128,1,64]{0,2,1:T(8,128)(2,1)S(1)}, u32[]{:S(2)}, u32[]{:S(2)}) collective-permute-start(bf16[128,1,64]{0,2,1:T(8,128)(2,1)S(1)} %get-tuple-element.54), channel_id=1, source_target_pairs={{0,2},{1,3},{2,4},{3,5},{4,6},{5,7},{6,0},{7,1},{8,10},{9,11},{10,... | collective-permute-start | bytes 49160 | tf_op jit(solution)/shard_map/ppermute | solution.py:30
  32.0 3.1 %all-to-all-done = bf16[128,8,128]{0,2,1:T(8,128)(2,1)S(1)} async-done(((bf16[128,8,128]{0,2,1:T(8,128)(2,1)}), bf16[128,8,128]{0,2,1:T(8,128)(2,1)S(1)}, u32[]{:S(2)}, u32[]{:S(2)}) %all-to-all-start) | async-done | bytes 262176 | tf_op jit(solution)/shard_map/all_to_all | solution.py:108
  35.0 3.4 %all-to-all-start.2 = ((bf16[128,8,64]{0,2,1:T(8,128)(2,1)}), bf16[128,8,64]{0,2,1:T(8,128)(2,1)S(1)}, u32[]{:S(2)}, u32[]{:S(2)}) async-start(bf16[128,8,64]{0,2,1:T(8,128)(2,1)} %bitcast.37), calls=%async_computation.2 | async-start | bytes 262144 | tf_op jit(solution)/shard_map/all_to_all | solution.py:109
  39.4 2.8 %collective-permute-start.2 = (bf16[128,1,64]{0,2,1:T(8,128)(2,1)S(1)}, bf16[128,1,64]{0,2,1:T(8,128)(2,1)S(1)}, u32[]{:S(2)}, u32[]{:S(2)}) collective-permute-start(bf16[128,1,64]{0,2,1:T(8,128)(2,1)S(1)} %get-tuple-element.53), channel_id=1, source_target_pairs={{0,3},{1,4},{2,5},{3,6},{4,7},{5,0},{6,1},{7,2},{8,11},{9,12},{10,... | collective-permute-start | bytes 49160 | tf_op jit(solution)/shard_map/ppermute | solution.py:30
  42.2 2.9 %collective-permute-done.2 = bf16[128,1,64]{0,2,1:T(8,128)(2,1)S(1)} collective-permute-done((bf16[128,1,64]{0,2,1:T(8,128)(2,1)S(1)}, bf16[128,1,64]{0,2,1:T(8,128)(2,1)S(1)}, u32[]{:S(2)}, u32[]{:S(2)}) %collective-permute-start.2) | collective-permute-done | bytes 16416 | tf_op jit(solution)/shard_map/ppermute | solution.py:30
  46.6 12.3 %all-gather.2.cloned.1.call-done = bf16[4096,1,128]{2,0,1:T(8,128)(2,1)} async-done(((bf16[1024,1,128]{2,0,1:T(8,128)(2,1)}), bf16[4096,1,128]{2,0,1:T(8,128)(2,1)}) %all-gather.2.cloned.1.call-update) | async-done | bytes 1048592 | tf_op jit(solution)/shard_map/all_gather | solution.py:111
  58.9 2.2 %gather_fusion = bf16[128,64,128]{2,1,0:T(8,128)(2,1)S(1)} fusion(bf16[64,64,128]{2,1,0:T(8,128)(2,1)} %bitcast.235, s32[1024]{0:T(1024)S(1)} %pad_clamp_fusion.1), kind=kCustom, calls=%fused_computation | custom fusion | bytes 4194816 | tf_op jit(solution)/shard_map/while/body/eval_jaxpr/gather | solution.py:36
  62.1 1.1 bitcast_reduce_fusion
  63.2 2.9 %fusion.32 = (f32[16,64]{1,0:T(8,128)S(1)}, bf16[16,64,1,64]{1,3,0,2:T(8,128)(2,1)}) fusion(f32[16,64,1,64]{1,0,3,2:T(8,128)S(1)} %reshape.230, f32[16,64]{1,0:T(8,128)S(1)} %bitcast_reduce_fusion, f32[16,64]{1,0:T(8,128)S(1)} %get-tuple-element.56, f32[16,8,64,64]{3,2,1,0:T(8,128)S(1)} %get-tuple-element.57, pred[16,8]{1,0:T(8,128)(4,1)S(1)} %iota_compare_fusion, ...), kind=kOutput, calls=%fused_computation.33 | convolution fusion | flops 69991424 | bytes 4599936 | tf_op jit(solution)/shard_map/while/body/eval_jaxpr/gqhjk,gjkhd->gqhd/dot_general | solution.py:51
  66.2 1.2 convolution_bitcast_fusion
  67.4 1.9 %fusion = bf16[16,64,1,8,64]{1,4,3,0,2:T(8,128)(2,1)S(1)} fusion(bf16[16,64,64,1]{2,1,3,0:T(8,128)(2,1)S(1)} %bitcast.260, f32[16,64]{1,0:T(8,128)S(1)} %get-tuple-element.58, f32[16,64]{1,0:T(8,128)S(1)} %bitcast_reduce_fusion, f32[16,64]{1,0:T(8,128)S(1)} %get-tuple-element.56, f32[16,8,64,64]{3,2,1,0:T(8,128)S(1)} %get-tuple-element.57, ...), kind=kOutput, calls=%fused_computation.5 | convolution fusion | flops 70778880 | bytes 5386368 | tf_op jit(solution)/shard_map/while/body/eval_jaxpr/gqhd,gjkhd->gqhjk/dot_general | solution.py:72
  71.1 3.1 %pad_maximum_fusion = f32[16,8,64,1,128]{4,2,1,0,3:T(8,128)} fusion(f32[16,8,64,1,64]{4,2,1,0,3:T(8,128)S(1)} %convolution_bitcast_fusion, f32[16,8,64,1,64]{4,2,1,0,3:T(8,128)S(1)} %multiply_bitcast_fusion), kind=kLoop, calls=%fused_computation.3 | loop fusion | flops 1048576 | bytes 8388608 | tf_op jit(solution)/shard_map/while/body/eval_jaxpr/concatenate | solution.py:94
  74.4 13.5 %scatter_fusion = f32[64,64,128]{2,1,0:T(8,128)S(1)} fusion(f32[64,64,128]{2,1,0:T(8,128)S(1)} %broadcast.137, s32[128]{0:T(128)S(1)} %reshape.235, f32[128,64,128]{2,1,0:T(8,128)} %bitcast.233), kind=kCustom, calls=%fused_computation.2 | custom fusion | flops 1048576 | bytes 12583424 | tf_op jit(solution)/shard_map/while/body/eval_jaxpr/scatter-add | solution.py:141
  88.0 1.3 copy-done
  90.2 2.3 %reduce.4 = bf16[1024,64]{1,0:T(8,128)(2,1)S(1)} reduce(bf16[1024,1,64]{2,1,0:T(2,128)(2,1)S(1)} %reshape.276, bf16[]{:T(256)} %broadcast.167), dimensions={1}, to_apply=%reshape.276.reduce_sub_computation | reduce | bytes 262146 | tf_op jit(solution)/shard_map/reshape | solution.py:149
  93.3 5.5 %all-to-all-start.1 = ((bf16[8,2,4096]{2,1,0:T(2,128)(2,1)}), bf16[8,2,4096]{2,1,0:T(2,128)(2,1)S(1)}, u32[]{:S(2)}, u32[]{:S(2)}) async-start(bf16[8,2,4096]{2,1,0:T(2,128)(2,1)} %reshape.278), calls=%async_computation.1 | async-start | bytes 262144 | tf_op jit(solution)/shard_map/all_to_all | solution.py:152
  98.9 3.1 %fusion.26 = bf16[16,64,1,64]{1,3,0,2:T(8,128)(2,1)S(1)} fusion(bf16[16,64,1,8,64]{1,4,3,0,2:T(8,128)(2,1)} %copy-done.1, bf16[16,8,64,1,128]{4,2,1,0,3:T(8,128)(2,1)} %bitcast.241), kind=kOutput, calls=%fused_computation.30 | convolution fusion | flops 67239936 | bytes 3276800 | tf_op jit(solution)/shard_map/while/body/eval_jaxpr/gqhjk,gjkhd->gqhd/dot_general | solution.py:77
  102.3 2.3 %reduce.5 = bf16[1024,64]{1,0:T(8,128)(2,1)S(1)} reduce(bf16[1024,1,64]{2,1,0:T(2,128)(2,1)S(1)} %reshape.277, bf16[]{:T(256)} %broadcast.167), dimensions={1}, to_apply=%reshape.277.reduce_sub_computation | reduce | bytes 262146 | tf_op jit(solution)/shard_map/reshape | solution.py:150
  106.3 5.2 %all-to-all-start.3 = ((bf16[8,2,4096]{2,1,0:T(2,128)(2,1)}), bf16[8,2,4096]{2,1,0:T(2,128)(2,1)S(1)}, u32[]{:S(2)}, u32[]{:S(2)}) async-start(bf16[8,2,4096]{2,1,0:T(2,128)(2,1)} %reshape.280), calls=%async_computation.3 | async-start | bytes 262144 | tf_op jit(solution)/shard_map/all_to_all | solution.py:153
  111.4 9.5 %reduce-scatter.2.cloned.1.call-done = f32[1024,1,128]{2,1,0:T(1,128)} async-done(((f32[4096,1,128]{2,1,0:T(1,128)}), f32[1024,1,128]{2,1,0:T(1,128)}) %reduce-scatter.2.cloned.1.call-update) | async-done | bytes 524304 | tf_op jit(solution)/shard_map/reduce_scatter | solution.py:147
  120.9 1.4 convert_element_type.61
  122.3 2.2 %reduce.6 = bf16[1024,128]{1,0:T(8,128)(2,1)S(1)} reduce(bf16[1024,1,128]{2,1,0:T(2,128)(2,1)S(1)} %convert_element_type.61, bf16[]{:T(256)} %broadcast.167), dimensions={1}, to_apply=%convert_element_type.61.reduce_sub_computation | reduce | bytes 524290 | tf_op jit(solution)/shard_map/convert_element_type | solution.py:148
  125.3 5.5 %all-to-all-start.4 = ((bf16[8,2,8192]{2,1,0:T(2,128)(2,1)}), bf16[8,2,8192]{2,1,0:T(2,128)(2,1)S(1)}, u32[]{:S(2)}, u32[]{:S(2)}) async-start(bf16[8,2,8192]{2,1,0:T(2,128)(2,1)} %reshape.282), calls=%async_computation.5 | async-start | bytes 524288 | tf_op jit(solution)/shard_map/all_to_all | solution.py:154
  133.8 6.0 %all-to-all-done.4 = bf16[8,2,8192]{2,1,0:T(2,128)(2,1)S(1)} async-done(((bf16[8,2,8192]{2,1,0:T(2,128)(2,1)}), bf16[8,2,8192]{2,1,0:T(2,128)(2,1)S(1)}, u32[]{:S(2)}, u32[]{:S(2)}) %all-to-all-start.4) | async-done | bytes 262176 | tf_op jit(solution)/shard_map/all_to_all | solution.py:154
  (76 shorter events, 17.9 us)
Async XLA Ops:
  8.3 36.9 %collective-permute-start.6 = (bf16[128,1,64]{0,2,1:T(8,128)(2,1)S(1)}, bf16[128,1,64]{0,2,1:T(8,128)(2,1)S(1)}, u32[]{:S(2)}, u32[]{:S(2)}) collective-permute-start(bf16[128,1,64]{0,2,1:T(8,128)(2,1)S(1)} %get-tuple-element.49), channel_id=1, source_target_pairs={{0,7},{1,0},{2,1},{3,2},{4,3},{5,4},{6,5},{7,6},{8,15},{9,8},{10,9... | collective-permute-start | bytes 49160 | tf_op jit(solution)/shard_map/ppermute | solution.py:30
  14.4 30.8 %collective-permute-start.5 = (bf16[128,1,64]{0,2,1:T(8,128)(2,1)S(1)}, bf16[128,1,64]{0,2,1:T(8,128)(2,1)S(1)}, u32[]{:S(2)}, u32[]{:S(2)}) collective-permute-start(bf16[128,1,64]{0,2,1:T(8,128)(2,1)S(1)} %get-tuple-element.50), channel_id=1, source_target_pairs={{0,6},{1,7},{2,0},{3,1},{4,2},{5,3},{6,4},{7,5},{8,14},{9,15},{10,... | collective-permute-start | bytes 49160 | tf_op jit(solution)/shard_map/ppermute | solution.py:30
  14.9 30.3 %collective-permute-start.4 = (bf16[128,1,64]{0,2,1:T(8,128)(2,1)S(1)}, bf16[128,1,64]{0,2,1:T(8,128)(2,1)S(1)}, u32[]{:S(2)}, u32[]{:S(2)}) collective-permute-start(bf16[128,1,64]{0,2,1:T(8,128)(2,1)S(1)} %get-tuple-element.51), channel_id=1, source_target_pairs={{0,5},{1,6},{2,7},{3,0},{4,1},{5,2},{6,3},{7,4},{8,13},{9,14},{10,... | collective-permute-start | bytes 49160 | tf_op jit(solution)/shard_map/ppermute | solution.py:30
  14.9 30.3 %collective-permute-start.3 = (bf16[128,1,64]{0,2,1:T(8,128)(2,1)S(1)}, bf16[128,1,64]{0,2,1:T(8,128)(2,1)S(1)}, u32[]{:S(2)}, u32[]{:S(2)}) collective-permute-start(bf16[128,1,64]{0,2,1:T(8,128)(2,1)S(1)} %get-tuple-element.52), channel_id=1, source_target_pairs={{0,4},{1,5},{2,6},{3,7},{4,0},{5,1},{6,2},{7,3},{8,12},{9,13},{10,... | collective-permute-start | bytes 49160 | tf_op jit(solution)/shard_map/ppermute | solution.py:30
  17.8 12.1 %collective-permute-start = (bf16[128,1,64]{0,2,1:T(8,128)(2,1)S(1)}, bf16[128,1,64]{0,2,1:T(8,128)(2,1)S(1)}, u32[]{:S(2)}, u32[]{:S(2)}) collective-permute-start(bf16[128,1,64]{0,2,1:T(8,128)(2,1)S(1)} %get-tuple-element.55), channel_id=1, source_target_pairs={{0,1},{1,2},{2,3},{3,4},{4,5},{5,6},{6,7},{7,0},{8,9},{9,10},{10,1... | collective-permute-start | bytes 49160 | tf_op jit(solution)/shard_map/ppermute | solution.py:30
  22.1 12.9 %all-to-all-start = ((bf16[128,8,128]{0,2,1:T(8,128)(2,1)}), bf16[128,8,128]{0,2,1:T(8,128)(2,1)S(1)}, u32[]{:S(2)}, u32[]{:S(2)}) async-start(bf16[128,8,128]{0,2,1:T(8,128)(2,1)} %pad_maximum_fusion.1), calls=%async_computation | async-start | bytes 524288 | tf_op jit(solution)/shard_map/all_to_all | solution.py:108
  29.9 9.5 %collective-permute-start.1 = (bf16[128,1,64]{0,2,1:T(8,128)(2,1)S(1)}, bf16[128,1,64]{0,2,1:T(8,128)(2,1)S(1)}, u32[]{:S(2)}, u32[]{:S(2)}) collective-permute-start(bf16[128,1,64]{0,2,1:T(8,128)(2,1)S(1)} %get-tuple-element.54), channel_id=1, source_target_pairs={{0,2},{1,3},{2,4},{3,5},{4,6},{5,7},{6,0},{7,1},{8,10},{9,11},{10,... | collective-permute-start | bytes 49160 | tf_op jit(solution)/shard_map/ppermute | solution.py:30
  35.0 11.0 %all-to-all-start.2 = ((bf16[128,8,64]{0,2,1:T(8,128)(2,1)}), bf16[128,8,64]{0,2,1:T(8,128)(2,1)S(1)}, u32[]{:S(2)}, u32[]{:S(2)}) async-start(bf16[128,8,64]{0,2,1:T(8,128)(2,1)} %bitcast.37), calls=%async_computation.2 | async-start | bytes 262144 | tf_op jit(solution)/shard_map/all_to_all | solution.py:109
  38.4 20.5 %all-gather.2.cloned.1.call-start = ((), (), s32[]{:S(2)}) async-start(), calls=%async_computation.6 | async-start | bytes 1310720 | tf_op jit(solution)/shard_map/all_gather | solution.py:111
  39.3 81.6 %reduce-scatter.2.cloned.1.call-start = ((), (), s32[]{:S(2)}) async-start(), calls=%async_computation.7 | async-start | bytes 2621440 | tf_op jit(solution)/shard_map/reduce_scatter | solution.py:147
  39.4 5.8 %collective-permute-start.2 = (bf16[128,1,64]{0,2,1:T(8,128)(2,1)S(1)}, bf16[128,1,64]{0,2,1:T(8,128)(2,1)S(1)}, u32[]{:S(2)}, u32[]{:S(2)}) collective-permute-start(bf16[128,1,64]{0,2,1:T(8,128)(2,1)S(1)} %get-tuple-element.53), channel_id=1, source_target_pairs={{0,3},{1,4},{2,5},{3,6},{4,7},{5,0},{6,1},{7,2},{8,11},{9,12},{10,... | collective-permute-start | bytes 49160 | tf_op jit(solution)/shard_map/ppermute | solution.py:30
  61.1 6.3 %copy-start.2 = (bf16[128,64,128]{2,1,0:T(8,128)(2,1)}, bf16[128,64,128]{2,1,0:T(8,128)(2,1)S(1)}, u32[]{:S(2)}) copy-start(bf16[128,64,128]{2,1,0:T(8,128)(2,1)S(1)} %gather_fusion) | copy-start | bytes 6291460
  69.3 1.4 copy-start.1
  74.4 14.9 %copy-start.3 = (bf16[16,64,1,64]{1,3,0,2:T(8,128)(2,1)S(1)}, bf16[16,64,1,64]{1,3,0,2:T(8,128)(2,1)}, u32[]{:S(2)}) copy-start(bf16[16,64,1,64]{1,3,0,2:T(8,128)(2,1)} %get-tuple-element.59) | copy-start | bytes 393220
  87.9 1.3 copy-start
  93.3 12.9 %all-to-all-start.1 = ((bf16[8,2,4096]{2,1,0:T(2,128)(2,1)}), bf16[8,2,4096]{2,1,0:T(2,128)(2,1)S(1)}, u32[]{:S(2)}, u32[]{:S(2)}) async-start(bf16[8,2,4096]{2,1,0:T(2,128)(2,1)} %reshape.278), calls=%async_computation.1 | async-start | bytes 262144 | tf_op jit(solution)/shard_map/all_to_all | solution.py:152
  106.3 19.0 %all-to-all-start.3 = ((bf16[8,2,4096]{2,1,0:T(2,128)(2,1)}), bf16[8,2,4096]{2,1,0:T(2,128)(2,1)S(1)}, u32[]{:S(2)}, u32[]{:S(2)}) async-start(bf16[8,2,4096]{2,1,0:T(2,128)(2,1)} %reshape.280), calls=%async_computation.3 | async-start | bytes 262144 | tf_op jit(solution)/shard_map/all_to_all | solution.py:153
  125.3 14.4 %all-to-all-start.4 = ((bf16[8,2,8192]{2,1,0:T(2,128)(2,1)}), bf16[8,2,8192]{2,1,0:T(2,128)(2,1)S(1)}, u32[]{:S(2)}, u32[]{:S(2)}) async-start(bf16[8,2,8192]{2,1,0:T(2,128)(2,1)} %reshape.282), calls=%async_computation.5 | async-start | bytes 524288 | tf_op jit(solution)/shard_map/all_to_all | solution.py:154
Sparse Core Ops, SparseCore 0:
  40.8 18.0 all-gather.1
  89.4 31.4 reduce-scatter.1
